TPU v7x, 32 devices: a whole 2x2x4 slice. The times are simulated.
32 devices in a mesh: grp: 2 (over y), pts: 8 (over z, x), rcv: 2 (over core).
Axes of the slice: x: 2, y: 2, z: 4, core: 2. Of those that a mesh axis runs over, the one named last changes fastest.
Arguments:
- src_green: float32 [2, 128, 2048], P(None, 'grp', 'pts'), parts along dimension 1, may hold values from -0.125 to 0.125
- rcv_green: float32 [2, 2048, 2048], P(None, ('grp', 'rcv'), 'pts'), parts along dimension 1, may hold values from -6 to 6
- model: float32 [4096], P(('grp', 'pts')), parts along dimension 0, may hold values from -6 to 6
- observed: float32 [128, 2, 1024], P(('grp', 'pts'), None, 'rcv'), parts along dimension 0, may hold values from -30 to 30, as said below
Outputs:
- gradient: float32 [4096], P(('grp', 'pts')), parts along dimension 0
There are 2 independent parts, one for each index of `grp`. A program takes and returns all parts, laid end to end along the dimension named above; each array names one. Nothing has to cross between parts.
Inputs may be any that keep to these rules, and one draw needn't show every extreme that they name: `observed`: complex data (real and imaginary parts) whose scale varies with the source.
All inputs are finite; a program needn't handle non-finite values.
Results may differ from a plain program's by a relative error of at most 0.000068.
Values sent between devices are 32-bit elements; how exact they have to be, the bound alone decides.
A program may use at most 64 MiB of HBM per device.

v0:
```python
import jax
import jax.numpy as jnp
from jax import lax
from jax.sharding import PartitionSpec as P


def modelled_data(scaled, rcv_green):
    highest = lax.Precision.HIGHEST
    real_part = jnp.dot(
        scaled[0], rcv_green[0].T, precision=highest, preferred_element_type=jnp.float32
    ) - jnp.dot(scaled[1], rcv_green[1].T, precision=highest, preferred_element_type=jnp.float32)
    imag_part = jnp.dot(
        scaled[0], rcv_green[1].T, precision=highest, preferred_element_type=jnp.float32
    ) + jnp.dot(scaled[1], rcv_green[0].T, precision=highest, preferred_element_type=jnp.float32)
    return jnp.stack([real_part, imag_part], axis=1)


def image_terms(weighted, rcv_green, src_rows):
    highest = lax.Precision.HIGHEST
    back_real = jnp.dot(
        weighted[:, 0, :], rcv_green[0], precision=highest, preferred_element_type=jnp.float32
    ) + jnp.dot(
        weighted[:, 1, :], rcv_green[1], precision=highest, preferred_element_type=jnp.float32
    )
    back_imag = jnp.dot(
        weighted[:, 1, :], rcv_green[0], precision=highest, preferred_element_type=jnp.float32
    ) - jnp.dot(
        weighted[:, 0, :], rcv_green[1], precision=highest, preferred_element_type=jnp.float32
    )
    return jnp.sum(src_rows[0] * back_real + src_rows[1] * back_imag, axis=0)


def cauchy_weights(resid, spread_sq):
    energy = resid[:, 0, :] ** 2 + resid[:, 1, :] ** 2
    return resid / (1.0 + energy / spread_sq)[:, None, :]


def local(src_green, rcv_green, model, observed):
    num_sources = src_green.shape[1]
    num_points = src_green.shape[2] * lax.axis_size("pts")
    num_receivers = rcv_green.shape[1] * lax.axis_size("rcv")
    scaled = src_green * model[None, None, :]
    all_observed = lax.all_gather(observed, "pts", axis=0, tiled=True)
    modelled = lax.psum(modelled_data(scaled, rcv_green), "pts")
    resid = modelled - all_observed
    energy_sum = jnp.sum(resid[:, 0, :] ** 2 + resid[:, 1, :] ** 2)
    total = lax.psum(energy_sum, "rcv")
    spread_sq = total / (num_sources * num_receivers) + 1e-06
    weighted = cauchy_weights(resid, spread_sq)
    partial_image = image_terms(weighted, rcv_green, src_green)
    image = lax.psum(partial_image, "rcv")
    return image * jnp.sqrt(jnp.float32(num_points) / (num_receivers * num_sources))


def solution(mesh):
    placed = (
        P(None, "grp", "pts"),
        P(None, ("grp", "rcv"), "pts"),
        P(("grp", "pts")),
        P(("grp", "pts"), None, "rcv"),
    )
    return jax.shard_map(
        local, mesh=mesh, in_specs=placed, out_specs=P(("grp", "pts")), check_vma=False
    )
```

profile of v0, /device:TPU:0, one launch (start us, length us, event | category | flops | bytes accessed | tf_op | source)
XLA Modules:
  0.0 104.5 jit_solution(12044138015975517374)
XLA Ops:
  6.5 0.0 copy-start
  6.5 0.0 all-reduce.2.cloned.1.call-start
  6.5 1.0 broadcast_multiply_fusion
  7.5 1.6 %fusion.16 = f32[64,512]{1,0:T(8,128)S(1)} fusion(f32[2,512,256]{2,1,0:T(8,128)} %param.5, f32[2,64,256]{2,1,0:T(8,128)S(1)} %broadcast_multiply_fusion), kind=kOutput, calls=%fused_computation.20 | convolution fusion | flops 100663296 | bytes 720896 | tf_op jit(solution)/shard_map/dot_general | solution.py:9
  9.2 1.6 %fusion.8 = f32[64,512]{1,0:T(8,128)S(1)} fusion(f32[2,512,256]{2,1,0:T(8,128)} %param.5, f32[2,64,256]{2,1,0:T(8,128)S(1)} %broadcast_multiply_fusion), kind=kOutput, calls=%fused_computation.12 | convolution fusion | flops 100663296 | bytes 720896 | tf_op jit(solution)/shard_map/dot_general | solution.py:12
  10.8 0.0 copy-done
  10.9 0.6 fusion.1
  11.5 0.6 fusion
  12.1 0.7 pad_maximum_fusion
  12.8 0.0 copy-start.2
  12.8 0.0 all-reduce.2.cloned.1.call-update
  12.8 0.7 copy-done.2
  13.6 32.6 %all_gather.3 = f32[64,2,512]{2,0,1:T(8,128)S(1)} all-gather(f32[8,2,512]{2,0,1:T(8,128)S(1)} %copy.5), channel_id=1, replica_groups=mesh['grp'=2,'pts'=8,'rcv'=2] {'pts'}, dimensions={0}, use_global_device_ids=true | all-gather | bytes 294912 | tf_op jit(solution)/shard_map/all_gather | solution.py:43
  46.1 40.9 %all-reduce.2.cloned.1.call-done = f32[64,2,512]{2,0,1:T(8,128)} async-done(((f32[64,2,512]{2,0,1:T(8,128)}), f32[64,2,512]{2,0,1:T(8,128)}) %all-reduce.2.cloned.1.call-update) | async-done | bytes 262160 | tf_op jit(solution)/shard_map/psum | solution.py:44
  87.1 1.0 sub.10
  88.1 0.6 fusion.27
  88.7 3.1 %psum.22 = f32[]{:T(128)} all-reduce(f32[]{:T(128)} %fusion.27), channel_id=1, replica_groups=mesh['grp'=2,'pts'=8,'rcv'=2] {'rcv'}, use_global_device_ids=true, to_apply=%region_2.0 | all-reduce | flops 1 | bytes 8 | tf_op jit(solution)/shard_map/psum | solution.py:47
  92.5 0.4 fusion.13
  92.9 0.0 copy-start.1
  92.9 0.4 fusion.11
  93.3 0.5 copy-done.1
  93.8 0.4 fusion.4
  94.2 0.4 fusion.5
  94.6 2.5 %psum.23 = f32[256]{0:T(256)S(1)} all-reduce(f32[256]{0:T(256)S(1)} %fusion.5), channel_id=1, replica_groups=mesh['grp'=2,'pts'=8,'rcv'=2] {'rcv'}, use_global_device_ids=true, to_apply=%region_4.0 | all-reduce | flops 256 | bytes 2048 | tf_op jit(solution)/shard_map/psum | solution.py:51
  97.0 0.6 broadcast_multiply_fusion.1
  (3 shorter events, 0.1 us)
Async XLA Ops:
  6.5 4.3 %copy-start = (f32[2,512,256]{2,1,0:T(8,128)S(1)}, f32[2,512,256]{2,1,0:T(8,128)}, u32[]{:S(2)}) copy-start(f32[2,512,256]{2,1,0:T(8,128)} %param.5) | copy-start | bytes 3145732
  6.5 80.5 %all-reduce.2.cloned.1.call-start = ((), (), s32[]{:S(2)}) async-start(), calls=%async_computation | async-start | bytes 524288 | tf_op jit(solution)/shard_map/psum | solution.py:44
  12.8 0.8 copy-start.2
  92.9 0.9 copy-start.1
Sparse Core Ops, SparseCore 0:
  12.9 74.0 all-reduce.1
where the time goes:
time: 105 us; the launch traced here: 104 us
  waiting for transfers between devices  40.9 us (39%)
  blocking collectives  38.1 us (36%)
  between operations  14.1 us (13%)
  matrix products  6.05 us (6%)
  other arithmetic  3.97 us (4%)
  local copies, waits for them, and re-layouts  1.26 us (1%)
    psum x1, waiting for transfers between devices, local(): modelled = lax.psum(modelled_data(scaled, rcv_green), 'pts')  40.9 us
    all_gather x1, blocking collectives, local(): all_observed = lax.all_gather(observed, 'pts', axis=0, tiled=True)  32.6 us
    psum x1, blocking collectives, local(): total = lax.psum(energy_sum, 'rcv')  3.08 us
    psum x1, blocking collectives, local(): image = lax.psum(partial_image, 'rcv')  2.47 us
  transfers between devices with their start and end apart: 1, of which 1 were waited for; matrix products, arithmetic and copies ran while one was open for 0% of the time, Pallas kernels for 0%

commit v1 on v0

--- a/solution.py
+++ b/solution.py
@@ -41,7 +41,7 @@
     num_receivers = rcv_green.shape[1] * lax.axis_size("rcv")
     scaled = src_green * model[None, None, :]
     all_observed = lax.all_gather(observed, "pts", axis=0, tiled=True)
-    modelled = lax.psum(modelled_data(scaled, rcv_green), "pts")
+    modelled = jnp.sum(lax.all_gather(modelled_data(scaled, rcv_green), "pts"), axis=0)
     resid = modelled - all_observed
     energy_sum = jnp.sum(resid[:, 0, :] ** 2 + resid[:, 1, :] ** 2)
     total = lax.psum(energy_sum, "rcv")

time: 105 us -> 84.4 us (0.80)
  waiting for transfers between devices: 40.9 us -> 19.4 us
  local copies, waits for them, and re-layouts: 1.26 us -> 0.02 us
    psum x1 -> x0, waiting for transfers between devices: 40.9 us -> none  [local(): modelled = lax.psum(modelled_data(scaled, rcv_green), 'pts')]
    all_gather x0 -> x1, waiting for transfers between devices: none -> 19.3 us  [local(): lax.all_gather(modelled_data(scaled, rcv_green), 'pts')]
    reduce_sum x0 -> x1, other arithmetic: none -> 1.82 us  [local(): jnp.sum(lax.all_gather(modelled_data(scaled, rcv_green), 'pts'), axis=0)]
    unnamed x7, local copies, waits for them, and re-layouts: 1.26 us -> 0.02 us
where the time goes in v1:
time: 84.4 us; the launch traced here: 84.1 us
  blocking collectives  38.6 us (46%)
  waiting for transfers between devices  19.4 us (23%)
  between operations  14.1 us (17%)
  matrix products  7.09 us (8%)
  other arithmetic  4.87 us (6%)
    all_gather x1, blocking collectives, local(): all_observed = lax.all_gather(observed, 'pts', axis=0, tiled=True)  33.1 us
    all_gather x1, waiting for transfers between devices, local(): lax.all_gather(modelled_data(scaled, rcv_green), 'pts')  19.3 us
    psum x1, blocking collectives, local(): total = lax.psum(energy_sum, 'rcv')  3.08 us
    psum x1, blocking collectives, local(): image = lax.psum(partial_image, 'rcv')  2.47 us
    reduce_sum x1, other arithmetic, local(): jnp.sum(lax.all_gather(modelled_data(scaled, rcv_green), 'pts'), axis=0)  1.82 us
  transfers between devices with their start and end apart: 1, of which 1 were waited for; matrix products, arithmetic and copies ran while one was open for 0% of the time, Pallas kernels for 0%

profile of v1, /device:TPU:0, one launch (start us, length us, event | category | flops | bytes accessed | tf_op | source)
XLA Modules:
  0.0 84.1 jit_solution(8579511648600364353)
XLA Ops:
  6.5 0.0 copy-start
  6.5 0.0 copy-start.2
  6.5 0.0 all-gather.3.cloned.1.call-start
  6.5 1.0 %broadcast_multiply_fusion = f32[2,64,256]{2,1,0:T(8,128)S(1)} fusion(f32[2,64,256]{2,1,0:T(8,128)} %param.4, f32[256]{0:T(256)} %param.6), kind=kLoop, calls=%fused_computation.40 | loop fusion | flops 32768 | bytes 263168 | tf_op jit(solution)/shard_map/mul | solution.py:42
  7.5 1.6 %fusion.16 = f32[64,512]{1,0:T(8,128)S(1)} fusion(f32[2,512,256]{2,1,0:T(8,128)} %param.5, f32[2,64,256]{2,1,0:T(8,128)S(1)} %broadcast_multiply_fusion), kind=kOutput, calls=%fused_computation.20 | convolution fusion | flops 100663296 | bytes 720896 | tf_op jit(solution)/shard_map/dot_general | solution.py:9
  9.2 1.6 %fusion.8 = f32[64,512]{1,0:T(8,128)S(1)} fusion(f32[2,512,256]{2,1,0:T(8,128)} %param.5, f32[2,64,256]{2,1,0:T(8,128)S(1)} %broadcast_multiply_fusion), kind=kOutput, calls=%fused_computation.12 | convolution fusion | flops 100663296 | bytes 720896 | tf_op jit(solution)/shard_map/dot_general | solution.py:12
  10.8 1.7 %fusion.1 = f32[64,1,512]{2,0,1:T(8,128)S(1)} fusion(f32[64,512]{1,0:T(8,128)S(1)} %fusion.16, f32[2,512,256]{2,1,0:T(8,128)} %param.5, f32[2,64,256]{2,1,0:T(8,128)S(1)} %broadcast_multiply_fusion), kind=kOutput, calls=%fused_computation.3 | convolution fusion | flops 100696064 | bytes 851968 | tf_op jit(solution)/shard_map/dot_general | solution.py:11
  12.5 0.0 copy-done
  12.5 0.6 fusion
  13.1 0.7 pad_maximum_fusion
  13.9 0.0 all-gather.3.cloned.1.call-update
  13.9 0.0 copy-done.2
  13.9 33.1 %all_gather.11 = f32[64,2,512]{2,0,1:T(8,128)S(1)} all-gather(f32[8,2,512]{2,0,1:T(8,128)S(1)} %copy.5), channel_id=1, replica_groups=mesh['grp'=2,'pts'=8,'rcv'=2] {'pts'}, dimensions={0}, use_global_device_ids=true | all-gather | bytes 294912 | tf_op jit(solution)/shard_map/all_gather | solution.py:43
  47.0 19.3 %all-gather.3.cloned.1.call-done = f32[512,2,512]{2,0,1:T(8,128)} async-done(((f32[64,2,512]{2,0,1:T(8,128)}), f32[512,2,512]{2,0,1:T(8,128)}) %all-gather.3.cloned.1.call-update) | async-done | bytes 2097168 | tf_op jit(solution)/shard_map/all_gather | solution.py:44
  66.3 1.8 %reduce_sum.27 = f32[64,2,512]{2,0,1:T(8,128)S(1)} reduce(f32[8,64,2,512]{3,1,0,2:T(8,128)} %bitcast.45, f32[]{:T(128)} %constant.1.clone.1), dimensions={0}, to_apply=%region_0.0 | reduce | flops 458752 | bytes 2359300 | tf_op jit(solution)/shard_map/reduce_sum | solution.py:44
  68.1 0.0 copy-start.1
  68.2 0.6 fusion.27
  68.8 3.1 %psum.14 = f32[]{:T(128)} all-reduce(f32[]{:T(128)} %fusion.27), channel_id=1, replica_groups=mesh['grp'=2,'pts'=8,'rcv'=2] {'rcv'}, use_global_device_ids=true, to_apply=%region_2.0 | all-reduce | flops 1 | bytes 8 | tf_op jit(solution)/shard_map/psum | solution.py:47
  72.6 0.4 fusion.13
  73.0 0.4 fusion.11
  73.4 0.0 copy-done.1
  73.4 0.4 fusion.4
  73.8 0.4 fusion.5
  74.2 2.5 %psum.15 = f32[256]{0:T(256)S(1)} all-reduce(f32[256]{0:T(256)S(1)} %fusion.5), channel_id=1, replica_groups=mesh['grp'=2,'pts'=8,'rcv'=2] {'rcv'}, use_global_device_ids=true, to_apply=%region_4.0 | all-reduce | flops 256 | bytes 2048 | tf_op jit(solution)/shard_map/psum | solution.py:51
  76.7 0.6 broadcast_multiply_fusion.1
  (4 shorter events, 0.1 us)
Async XLA Ops:
  6.5 6.0 %copy-start = (f32[2,512,256]{2,1,0:T(8,128)S(1)}, f32[2,512,256]{2,1,0:T(8,128)}, u32[]{:S(2)}) copy-start(f32[2,512,256]{2,1,0:T(8,128)} %param.5) | copy-start | bytes 3145732
  6.5 7.4 %copy-start.2 = (f32[8,2,512]{2,1,0:T(2,128)S(1)}, f32[8,2,512]{2,1,0:T(2,128)}, u32[]{:S(2)}) copy-start(f32[8,2,512]{2,1,0:T(2,128)} %param.7) | copy-start | bytes 98308
  6.5 59.8 %all-gather.3.cloned.1.call-start = ((), (), s32[]{:S(2)}) async-start(), calls=%async_computation | async-start | bytes 2359296 | tf_op jit(solution)/shard_map/all_gather | solution.py:44
  68.1 5.3 %copy-start.1 = (f32[2,64,256]{2,1,0:T(8,128)S(1)}, f32[2,64,256]{2,1,0:T(8,128)}, u32[]{:S(2)}) copy-start(f32[2,64,256]{2,1,0:T(8,128)} %param.4) | copy-start | bytes 393220
Sparse Core Ops, SparseCore 0:
  14.0 52.2 all-gather.2
